TPU v7x, 32 devices: a whole 2x2x4 slice. The times are simulated.
32 devices in a mesh: gx: 2 (over x), gy: 4 (over y, core), gz: 4 (over z).
Axes of the slice: x: 2, y: 2, z: 4, core: 2. Of those that a mesh axis runs over, the one named last changes fastest.
Arguments:
- panel: float32 [128, 131072], P(None, ('gx', 'gy', 'gz')), may hold values from -3000 to 3000
- trailing: float32 [64, 131072], P(None, ('gx', 'gy', 'gz')), may hold values from -6 to 6
Outputs:
- basis: float32 [128, 131072], P(None, ('gx', 'gy', 'gz'))
- upper: float32 [128, 128], replicated
- coupling: float32 [128, 64], replicated
- updated: float32 [64, 131072], P(None, ('gx', 'gy', 'gz'))
All inputs are finite; a program needn't handle non-finite values.
Results may differ from a plain program's by a relative error of at most 0.0033.
Values sent between devices are 32-bit elements; how exact they have to be, the bound alone decides.
A program may use at most 64 MiB of HBM per device.

v0:
```python
import functools

import jax
import jax.numpy as jnp
from jax import lax
from jax.experimental import pallas as pl
from jax.experimental.pallas import tpu as pltpu
from jax.sharding import PartitionSpec as P

MESH = pl.DeviceIdType.MESH
HIGHEST = lax.Precision.HIGHEST
NT = (((1,), (1,)), ((), ()))
NN = (((1,), (0,)), ((), ()))
VMEM = pl.BlockSpec(memory_space=pltpu.VMEM)
ANY = pl.BlockSpec(memory_space=pl.ANY)


def exact(left, right, dims):
    return lax.dot_general(left, right, dims, precision=HIGHEST, preferred_element_type=jnp.float32)


def halves(value):
    high = value.astype(jnp.bfloat16)
    return high, (value - high.astype(jnp.float32)).astype(jnp.bfloat16)


def three_pass(left, right, dims):
    dot = functools.partial(lax.dot_general, dimension_numbers=dims, preferred_element_type=jnp.float32)
    return dot(left[0], right[1]) + dot(left[1], right[0]) + dot(left[0], right[0])


def factor(tiles):
    size = tiles[0].shape[1]
    lane = lax.broadcasted_iota(jnp.int32, (1, size), 1)
    row_in_tile = lax.broadcasted_iota(jnp.int32, (8, 1), 0)
    lanes = lax.broadcasted_iota(jnp.int32, (8, size), 1)
    tiles = list(tiles)
    for k in range(size):
        at, r = divmod(k, 8)
        row = tiles[at][r : r + 1, :]
        here = lanes == k
        scaled = jnp.where(lane == k, 1.0, row) * (1.0 / row[:, k : k + 1])
        for h in range(at, len(tiles)):
            if h == at and r == 7:
                continue
            tile = tiles[h]
            new = jnp.where(here, 0.0, tile) - tile[:, k : k + 1] * scaled
            tiles[h] = jnp.where(row_in_tile > r, new, tile) if h == at else new
    uppers, inverses = [], []
    for h, tile in enumerate(tiles):
        rows = row_in_tile + 8 * h
        pivot = jnp.sum(jnp.where(lanes == rows, tile, 0.0), axis=1, keepdims=True)
        root = jnp.sqrt(pivot)
        over = 1.0 / root
        uppers.append(jnp.where(lanes > rows, tile * over, jnp.where(lanes == rows, root, 0.0)))
        inverses.append(jnp.where(lanes < rows, tile * over, jnp.where(lanes == rows, over, 0.0)))
    return uppers, inverses


def greet(sizes):
    nx, ny, nz = sizes
    gx, gy, gz = lax.axis_index("gx"), lax.axis_index("gy"), lax.axis_index("gz")
    barrier = pltpu.get_barrier_semaphore()
    me = gx * ny + gy
    for step in range(1, nx * ny):
        peer = lax.rem(me + step, nx * ny)
        pl.semaphore_signal(barrier, inc=1, device_id=(peer // ny, lax.rem(peer, ny), gz), device_id_type=MESH)
    for step in range(1, nz):
        pl.semaphore_signal(barrier, inc=1, device_id=(gx, gy, lax.rem(gz + step, nz)), device_id_type=MESH)


def all_sum(sizes, send, landed, column, gathered, send_sem, recv_sem):
    nx, ny, nz = sizes
    group = nx * ny
    gx, gy, gz = lax.axis_index("gx"), lax.axis_index("gy"), lax.axis_index("gz")
    me = gx * ny + gy
    pl.semaphore_wait(pltpu.get_barrier_semaphore(), group - 1 + nz - 1)

    def plane_copy(src, dst, step, base):
        peer = lax.rem(me + step, group)
        return pltpu.make_async_remote_copy(
            src_ref=src(peer),
            dst_ref=dst,
            send_sem=send_sem.at[base + step],
            recv_sem=recv_sem.at[base + step],
            device_id=(peer // ny, lax.rem(peer, ny), gz),
            device_id_type=MESH,
        )

    out = [plane_copy(lambda peer: send.at[peer], landed.at[step], step, 0) for step in range(1, group)]
    for copy in out:
        copy.start()
    part = send[me]
    for step in range(1, group):
        out[step - 1].wait_recv()
        part = part + landed[step]
    column[gz] = part
    along = [
        pltpu.make_async_remote_copy(
            src_ref=column.at[gz],
            dst_ref=column.at[gz],
            send_sem=send_sem.at[group + step],
            recv_sem=recv_sem.at[group + step],
            device_id=(gx, gy, lax.rem(gz + step, nz)),
            device_id_type=MESH,
        )
        for step in range(1, nz)
    ]
    for copy in along:
        copy.start()
    for copy in along:
        copy.wait_recv()
    total = column[0]
    for z in range(1, nz):
        total = total + column[z]
    gathered[me] = total
    back = [plane_copy(lambda peer: gathered.at[me], gathered.at[me], step, group + nz) for step in range(1, group)]
    for copy in back:
        copy.start()
    for copy in back:
        copy.wait_recv()
    for copy in out + along + back:
        copy.wait_send()


def sum_scratch(sizes, rows, size):
    nx, ny, nz = sizes
    group = nx * ny
    return [
        pltpu.VMEM((group, rows, size), jnp.float32),
        pltpu.VMEM((group, rows, size), jnp.float32),
        pltpu.VMEM((nz, rows, size), jnp.float32),
        pltpu.SemaphoreType.DMA((2 * group + nz,)),
        pltpu.SemaphoreType.DMA((2 * group + nz,)),
    ]


def chunk_of(width):
    return 512 if width % 512 == 0 else width


def gram_kernel(sizes, panel, gathered, send, landed, column, send_sem, recv_sem):
    greet(sizes)
    size, width = panel.shape
    chunk = chunk_of(width)

    def body(i, total):
        part = panel[:, pl.ds(pl.multiple_of(i * chunk, chunk), chunk)]
        return total + exact(part, part, NT)

    gram = lax.fori_loop(0, width // chunk, body, jnp.zeros((size, size), jnp.float32))
    group = sizes[0] * sizes[1]
    rows = size // group
    for p in range(group):
        send[p] = gram[p * rows : (p + 1) * rows]
    all_sum(sizes, send, landed, column, gathered, send_sem, recv_sem)


def factor_kernel(gram, upper, inverse):
    uppers, inverses = factor([gram[h : h + 8] for h in range(0, gram.shape[0], 8)])
    for h in range(len(uppers)):
        upper[8 * h : 8 * h + 8] = uppers[h]
        inverse[8 * h : 8 * h + 8] = inverses[h]


def apply_kernel(sizes, inverse, panel, trailing, first, gathered, send, landed, column, send_sem, recv_sem):
    greet(sizes)
    size, width = panel.shape
    trail = trailing.shape[0]
    chunk = chunk_of(width)
    inv = inverse[...]

    def body(i, totals):
        at = pl.ds(pl.multiple_of(i * chunk, chunk), chunk)
        basis = exact(inv, panel[:, at], NN)
        first[:, at] = basis
        high, low = halves(basis)
        own, cross = totals
        own = own + three_pass((high, low), (high, low), NT)
        cross = cross + three_pass(halves(trailing[:, at]), (high, low), NT)
        return own, cross

    start = (jnp.zeros((size, size), jnp.float32), jnp.zeros((trail, size), jnp.float32))
    own, cross = lax.fori_loop(0, width // chunk, body, start)
    group = sizes[0] * sizes[1]
    rows, less = size // group, trail // group
    for p in range(group):
        send[p, :rows] = own[p * rows : (p + 1) * rows]
        send[p, rows:] = cross[p * less : (p + 1) * less]
    all_sum(sizes, send, landed, column, gathered, send_sem, recv_sem)


def final_kernel(scale, gram, cross, upper_one, first, trailing, basis, upper, coupling, updated):
    size, width = first.shape
    uppers, inverses = factor([gram[h : h + 8] for h in range(0, size, 8)])
    inv = jnp.concatenate(inverses, axis=0)
    up = jnp.concatenate(uppers, axis=0)
    upper[...] = exact(up, upper_one[...], NN) * (1.0 / scale)
    coupling[...] = exact(inv, cross[...], NT)
    back = exact(exact(cross[...], inv, NT), inv, NN)
    scaled_inv, back = halves(inv * scale), halves(back)
    chunk = chunk_of(width)

    @pl.loop(0, width // chunk)
    def _(i):
        at = pl.ds(pl.multiple_of(i * chunk, chunk), chunk)
        part = halves(first[:, at])
        basis[:, at] = three_pass(scaled_inv, part, NN)
        updated[:, at] = trailing[:, at] - three_pass(back, part, NN)


def shards(sizes, panel, trailing):
    size, width = panel.shape
    trail = trailing.shape[0]
    nx, ny, nz = sizes
    group = nx * ny
    rows, less = size // group, trail // group
    f32 = jnp.float32
    scale = float(width * group * nz) ** 0.5

    def params(identity=None):
        return pltpu.CompilerParams(collective_id=identity, has_side_effects=identity is not None, vmem_limit_bytes=48 * 2**20)

    gram = pl.pallas_call(
        functools.partial(gram_kernel, sizes),
        out_shape=jax.ShapeDtypeStruct((group, rows, size), f32),
        in_specs=[VMEM],
        out_specs=VMEM,
        scratch_shapes=sum_scratch(sizes, rows, size),
        compiler_params=params(0),
        name="gram",
    )(panel)
    upper_one, inverse_one = pl.pallas_call(
        factor_kernel,
        out_shape=[jax.ShapeDtypeStruct((size, size), f32)] * 2,
        in_specs=[VMEM],
        out_specs=[VMEM] * 2,
        compiler_params=params(),
        name="factor",
    )(gram.reshape(size, size))
    first, summed = pl.pallas_call(
        functools.partial(apply_kernel, sizes),
        out_shape=[jax.ShapeDtypeStruct((size, width), f32), jax.ShapeDtypeStruct((group, rows + less, size), f32)],
        in_specs=[VMEM] * 3,
        out_specs=[VMEM] * 2,
        scratch_shapes=sum_scratch(sizes, rows + less, size),
        compiler_params=params(1),
        name="apply",
    )(inverse_one, panel, trailing)
    return pl.pallas_call(
        functools.partial(final_kernel, scale),
        out_shape=[
            jax.ShapeDtypeStruct((size, width), f32),
            jax.ShapeDtypeStruct((size, size), f32),
            jax.ShapeDtypeStruct((size, trail), f32),
            jax.ShapeDtypeStruct((trail, width), f32),
        ],
        in_specs=[VMEM] * 5,
        out_specs=[VMEM] * 4,
        compiler_params=params(),
        name="final",
    )(summed[:, :rows].reshape(size, size), summed[:, rows:].reshape(trail, size), upper_one, first, trailing)


def solution(mesh):
    sizes = tuple(mesh.shape[name] for name in ("gx", "gy", "gz"))
    placed = P(None, ("gx", "gy", "gz"))
    return jax.shard_map(
        functools.partial(shards, sizes),
        mesh=mesh,
        in_specs=(placed, placed),
        out_specs=(placed, P(), P(), placed),
        check_vma=False,
    )
```

profile of v0, /device:TPU:0, one launch (start us, length us, event | category | flops | bytes accessed | tf_op | source)
XLA Modules:
  0.0 62.7 jit_solution(17801580114083987585)
XLA Ops:
  0.6 0.0 copy-start
  0.6 1.6 %copy-done = f32[128,4096]{1,0:T(8,128)S(1)} copy-done((f32[128,4096]{1,0:T(8,128)S(1)}, f32[128,4096]{1,0:T(8,128)}, u32[]{:S(2)}) %copy-start) | copy-done | bytes 2097176
  2.2 0.0 copy-start.1
  2.2 16.8 %gram.1 = f32[8,16,128]{2,1,0:T(8,128)S(1)} custom-call(f32[128,4096]{1,0:T(8,128)S(1)} %copy-done), custom_call_target="tpu_custom_call" | custom-call | tf_op jit(solution)/shard_map/gram/pallas_call | solution.py:224
  19.0 10.8 %factor.1 = (f32[128,128]{1,0:T(8,128)S(1)}, f32[128,128]{1,0:T(8,128)S(1)}) custom-call(f32[128,128]{1,0:T(8,128)S(1)} %bitcast.5), custom_call_target="tpu_custom_call" | custom-call | tf_op jit(solution)/shard_map/factor/pallas_call | solution.py:233
  29.8 0.0 copy-done.1
  29.8 0.0 copy-start.2
  29.8 1.2 %copy-done.2 = f32[64,4096]{1,0:T(8,128)S(1)} copy-done((f32[64,4096]{1,0:T(8,128)S(1)}, f32[64,4096]{1,0:T(8,128)}, u32[]{:S(2)}) %copy-start.2) | copy-done | bytes 1048600
  31.1 0.0 copy-start.3
  31.1 15.4 %apply.1 = (f32[128,4096]{1,0:T(8,128)S(1)}, f32[8,24,128]{2,1,0:T(8,128)S(1)}) custom-call(f32[128,128]{1,0:T(8,128)S(1)} %get-tuple-element.8.inverse, f32[128,4096]{1,0:T(8,128)S(1)} %copy-done.1, f32[64,4096]{1,0:T(8,128)S(1)} %copy-done.2), custom_call_target="tpu_custom_call" | custom-call | tf_op jit(solution)/shard_map/apply/pallas_call | solution.py:241
  46.5 0.0 copy-done.3
  46.5 15.5 %final.1 = (f32[128,4096]{1,0:T(8,128)}, f32[128,128]{1,0:T(8,128)}, f32[128,64]{1,0:T(8,128)S(1)}, f32[64,4096]{1,0:T(8,128)}) custom-call(f32[128,128]{1,0:T(8,128)S(1)} %bitcast.4, f32[64,128]{1,0:T(8,128)S(1)} %slice_bitcast_fusion.cross, f32[128,128]{1,0:T(8,128)S(1)} %get-tuple-element.10.upper_one, f32[128,4096]{1,0:T(8,128)S(1)} %get-tuple-element.11.first, ...), custom_call_target="tpu_custom_call" | custom-call | tf_op jit(solution)/shard_map/final/pallas_call | solution.py:250
  62.0 0.7 %copy.6 = f32[128,64]{0,1:T(8,128)} copy(f32[128,64]{1,0:T(8,128)S(1)} %get-tuple-element.14) | data formatting | bytes 65536 | tf_op jit(solution)/shard_map/final/pallas_call | solution.py:250
  (2 shorter events, 0.0 us)
Async XLA Ops:
  0.6 1.6 %copy-start = (f32[128,4096]{1,0:T(8,128)S(1)}, f32[128,4096]{1,0:T(8,128)}, u32[]{:S(2)}) copy-start(f32[128,4096]{1,0:T(8,128)} %panel.3) | copy-start | bytes 6291460
  2.2 27.6 %copy-start.1 = (f32[128,4096]{1,0:T(8,128)S(1)}, f32[128,4096]{1,0:T(8,128)}, u32[]{:S(2)}) copy-start(f32[128,4096]{1,0:T(8,128)} %panel.3) | copy-start | bytes 6291460
  29.8 1.2 %copy-start.2 = (f32[64,4096]{1,0:T(8,128)S(1)}, f32[64,4096]{1,0:T(8,128)}, u32[]{:S(2)}) copy-start(f32[64,4096]{1,0:T(8,128)} %trailing.3) | copy-start | bytes 3145732
  31.1 15.4 %copy-start.3 = (f32[64,4096]{1,0:T(8,128)S(1)}, f32[64,4096]{1,0:T(8,128)}, u32[]{:S(2)}) copy-start(f32[64,4096]{1,0:T(8,128)} %trailing.3) | copy-start | bytes 3145732
where the time goes:
time: 62.9 us; the launch traced here: 62.7 us
  Pallas kernels  58.4 us (93%)
  local copies, waits for them, and re-layouts  3.53 us (6%)
  between operations  0.69 us (1%)
    pallas_call x1, Pallas kernels, shards(): pl.pallas_call(functools.partial(gram_kernel, sizes), out_shape=jax.Shape...  16.8 us
    pallas_call x1, Pallas kernels, shards(): pl.pallas_call(functools.partial(final_kernel, scale), out_shape=[jax.Sha...  15.5 us
    pallas_call x1, Pallas kernels, shards(): pl.pallas_call(functools.partial(apply_kernel, sizes), out_shape=[jax.Sha...  15.4 us
    pallas_call x1, Pallas kernels, shards(): pl.pallas_call(factor_kernel, out_shape=[jax.ShapeDtypeStruct((size, size...  10.8 us
    unnamed x8, local copies, waits for them, and re-layouts  2.82 us

commit v1 on v0

--- a/solution.py
+++ b/solution.py
@@ -12,21 +12,24 @@
 NT = (((1,), (1,)), ((), ()))
 NN = (((1,), (0,)), ((), ()))
 VMEM = pl.BlockSpec(memory_space=pltpu.VMEM)
-ANY = pl.BlockSpec(memory_space=pl.ANY)
+HBM = pl.BlockSpec(memory_space=pltpu.HBM)
 
 
 def exact(left, right, dims):
     return lax.dot_general(left, right, dims, precision=HIGHEST, preferred_element_type=jnp.float32)
 
 
-def halves(value):
-    high = value.astype(jnp.bfloat16)
-    return high, (value - high.astype(jnp.float32)).astype(jnp.bfloat16)
-
-
-def three_pass(left, right, dims):
-    dot = functools.partial(lax.dot_general, dimension_numbers=dims, preferred_element_type=jnp.float32)
-    return dot(left[0], right[1]) + dot(left[1], right[0]) + dot(left[0], right[0])
+def terms(value, count):
+    found = []
+    for _ in range(count):
+        term = value.astype(jnp.bfloat16)
+        found.append(term)
+        value = value - term.astype(jnp.float32)
+    return found
+
+
+def stacked(left, right, dims):
+    return lax.dot_general(left, right, dims, preferred_element_type=jnp.float32)
 
 
 def factor(tiles):
@@ -35,17 +38,30 @@
     row_in_tile = lax.broadcasted_iota(jnp.int32, (8, 1), 0)
     lanes = lax.broadcasted_iota(jnp.int32, (8, size), 1)
     tiles = list(tiles)
-    for k in range(size):
-        at, r = divmod(k, 8)
-        row = tiles[at][r : r + 1, :]
-        here = lanes == k
-        scaled = jnp.where(lane == k, 1.0, row) * (1.0 / row[:, k : k + 1])
-        for h in range(at, len(tiles)):
-            if h == at and r == 7:
-                continue
-            tile = tiles[h]
-            new = jnp.where(here, 0.0, tile) - tile[:, k : k + 1] * scaled
-            tiles[h] = jnp.where(row_in_tile > r, new, tile) if h == at else new
+    for at in range(len(tiles)):
+        first = 8 * at
+        inside = (lane >= first) & (lane < first + 8)
+        columns = {h: [jnp.broadcast_to(tiles[h][:, first + j : first + j + 1], (8, size)) for j in range(8)] for h in range(at, len(tiles))}
+        for h in range(at + 1, len(tiles)):
+            tiles[h] = jnp.where(inside, 0.0, tiles[h])
+        for r in range(8):
+            k = first + r
+            row = tiles[at][r : r + 1, :]
+            unit = jnp.where(lane == k, 1.0, row)
+            behind = jnp.where(inside & (lane > k), 0.0, unit)
+            pivots = [columns[at][j][r : r + 1, :] for j in range(8)]
+            over = 1.0 / pivots[r]
+            for h in range(at, len(tiles)):
+                if h == at and r == 7:
+                    continue
+                times = columns[h][r] * over
+                for j in range(r + 1, 8):
+                    columns[h][j] = columns[h][j] - times * pivots[j]
+                if h == at:
+                    below = row_in_tile > r
+                    tiles[h] = jnp.where(below, jnp.where(lanes == k, 0.0, tiles[h]) - times * unit, tiles[h])
+                else:
+                    tiles[h] = tiles[h] - times * behind
     uppers, inverses = [], []
     for h, tile in enumerate(tiles):
         rows = row_in_tile + 8 * h
@@ -135,20 +151,29 @@
     ]
 
 
-def chunk_of(width):
-    return 512 if width % 512 == 0 else width
-
-
-def gram_kernel(sizes, panel, gathered, send, landed, column, send_sem, recv_sem):
+def chunk_of(width, most):
+    return most if width % most == 0 else width
+
+
+def gram_kernel(sizes, panel, gathered, held, load_sem, send, landed, column, send_sem, recv_sem):
+    size, width = panel.shape
+    chunk = chunk_of(width, 1024)
+    loads = []
+    for i in range(width // chunk):
+        at = pl.ds(i * chunk, chunk)
+        loads.append(pltpu.make_async_copy(panel.at[:, at], held.at[:, at], load_sem.at[i]))
+        loads[-1].start()
     greet(sizes)
-    size, width = panel.shape
-    chunk = chunk_of(width)
-
-    def body(i, total):
-        part = panel[:, pl.ds(pl.multiple_of(i * chunk, chunk), chunk)]
-        return total + exact(part, part, NT)
-
-    gram = lax.fori_loop(0, width // chunk, body, jnp.zeros((size, size), jnp.float32))
+    both = jnp.zeros((2 * size, 2 * size), jnp.float32)
+    small = jnp.zeros((size, size), jnp.float32)
+    for i in range(width // chunk):
+        loads[i].wait()
+        high, middle, low = terms(held[:, i * chunk : (i + 1) * chunk], 3)
+        pair = jnp.concatenate([high, middle], axis=0)
+        both = both + stacked(pair, pair, NT)
+        small = small + stacked(high, low, NT)
+    small = small + both[:size, size:]
+    gram = both[:size, :size] + ((small + small.T) + both[size:, size:])
     group = sizes[0] * sizes[1]
     rows = size // group
     for p in range(group):
@@ -156,32 +181,39 @@
     all_sum(sizes, send, landed, column, gathered, send_sem, recv_sem)
 
 
-def factor_kernel(gram, upper, inverse):
+def factor_kernel(gram, trailing, upper, inverse, near, load_sem):
+    load = pltpu.make_async_copy(trailing, near, load_sem)
+    load.start()
     uppers, inverses = factor([gram[h : h + 8] for h in range(0, gram.shape[0], 8)])
     for h in range(len(uppers)):
         upper[8 * h : 8 * h + 8] = uppers[h]
         inverse[8 * h : 8 * h + 8] = inverses[h]
+    load.wait()
 
 
 def apply_kernel(sizes, inverse, panel, trailing, first, gathered, send, landed, column, send_sem, recv_sem):
     greet(sizes)
     size, width = panel.shape
     trail = trailing.shape[0]
-    chunk = chunk_of(width)
-    inv = inverse[...]
-
-    def body(i, totals):
+    chunk = chunk_of(width, 1024)
+    one, two, three = terms(inverse[...], 3)
+    left = jnp.concatenate([three, one, two, two, one, one], axis=1)
+
+    def body(i, total):
         at = pl.ds(pl.multiple_of(i * chunk, chunk), chunk)
-        basis = exact(inv, panel[:, at], NN)
+        high, middle, low = terms(panel[:, at], 3)
+        basis = stacked(left, jnp.concatenate([high, low, middle, high, middle, high], axis=0), NN)
         first[:, at] = basis
-        high, low = halves(basis)
-        own, cross = totals
-        own = own + three_pass((high, low), (high, low), NT)
-        cross = cross + three_pass(halves(trailing[:, at]), (high, low), NT)
-        return own, cross
-
-    start = (jnp.zeros((size, size), jnp.float32), jnp.zeros((trail, size), jnp.float32))
-    own, cross = lax.fori_loop(0, width // chunk, body, start)
+        high, low = terms(basis, 2)
+        c_high, c_low = terms(trailing[:, at], 2)
+        pairs = stacked(jnp.concatenate([high, c_high, c_low], axis=0), jnp.concatenate([high, low], axis=0), NT)
+        return total + pairs
+
+    total = lax.fori_loop(0, width // chunk, body, jnp.zeros((size + 2 * trail, 2 * size), jnp.float32))
+    mixed = total[:size, size:]
+    own = total[:size, :size] + (mixed + mixed.T)
+    cross = total[size:, :size] + total[size:, size:]
+    cross = cross[:trail] + cross[trail:]
     group = sizes[0] * sizes[1]
     rows, less = size // group, trail // group
     for p in range(group):
@@ -190,23 +222,30 @@
     all_sum(sizes, send, landed, column, gathered, send_sem, recv_sem)
 
 
-def final_kernel(scale, gram, cross, upper_one, first, trailing, basis, upper, coupling, updated):
+def final_kernel(scale, gram, cross, upper_one, first, trailing, basis, upper, coupling, updated, basis_held, updated_held, store_sem):
     size, width = first.shape
     uppers, inverses = factor([gram[h : h + 8] for h in range(0, size, 8)])
     inv = jnp.concatenate(inverses, axis=0)
     up = jnp.concatenate(uppers, axis=0)
+    mixed = exact(cross[...], inv, NT)
+    coupling[...] = mixed
+    both = jnp.concatenate([inv * scale, exact(mixed, inv, NN)], axis=0)
+    high, low = terms(both, 2)
+    left = jnp.concatenate([low, low, high, high], axis=1)
+    chunk = chunk_of(width, 512)
+    stores = []
+    for i in range(width // chunk):
+        at = pl.ds(i * chunk, chunk)
+        high, low = terms(first[:, at], 2)
+        out = stacked(left, jnp.concatenate([low, high, low, high], axis=0), NN)
+        basis_held[:, at] = out[:size]
+        updated_held[:, at] = trailing[:, at] - out[size:]
+        for place, (src, dst) in enumerate(((basis_held, basis), (updated_held, updated))):
+            stores.append(pltpu.make_async_copy(src.at[:, at], dst.at[:, at], store_sem.at[place, i]))
+            stores[-1].start()
     upper[...] = exact(up, upper_one[...], NN) * (1.0 / scale)
-    coupling[...] = exact(inv, cross[...], NT)
-    back = exact(exact(cross[...], inv, NT), inv, NN)
-    scaled_inv, back = halves(inv * scale), halves(back)
-    chunk = chunk_of(width)
-
-    @pl.loop(0, width // chunk)
-    def _(i):
-        at = pl.ds(pl.multiple_of(i * chunk, chunk), chunk)
-        part = halves(first[:, at])
-        basis[:, at] = three_pass(scaled_inv, part, NN)
-        updated[:, at] = trailing[:, at] - three_pass(back, part, NN)
+    for store in stores:
+        store.wait()
 
 
 def shards(sizes, panel, trailing):
@@ -224,20 +263,25 @@
     gram = pl.pallas_call(
         functools.partial(gram_kernel, sizes),
         out_shape=jax.ShapeDtypeStruct((group, rows, size), f32),
-        in_specs=[VMEM],
+        in_specs=[HBM],
         out_specs=VMEM,
-        scratch_shapes=sum_scratch(sizes, rows, size),
+        scratch_shapes=[
+            pltpu.VMEM((size, width), f32),
+            pltpu.SemaphoreType.DMA((width // chunk_of(width, 1024),)),
+            *sum_scratch(sizes, rows, size),
+        ],
         compiler_params=params(0),
         name="gram",
     )(panel)
-    upper_one, inverse_one = pl.pallas_call(
+    upper_one, inverse_one, near = pl.pallas_call(
         factor_kernel,
-        out_shape=[jax.ShapeDtypeStruct((size, size), f32)] * 2,
-        in_specs=[VMEM],
-        out_specs=[VMEM] * 2,
+        out_shape=[jax.ShapeDtypeStruct((size, size), f32)] * 2 + [jax.ShapeDtypeStruct((trail, width), f32)],
+        in_specs=[VMEM, HBM],
+        out_specs=[VMEM] * 3,
+        scratch_shapes=[pltpu.SemaphoreType.DMA],
         compiler_params=params(),
         name="factor",
-    )(gram.reshape(size, size))
+    )(gram.reshape(size, size), trailing)
     first, summed = pl.pallas_call(
         functools.partial(apply_kernel, sizes),
         out_shape=[jax.ShapeDtypeStruct((size, width), f32), jax.ShapeDtypeStruct((group, rows + less, size), f32)],
@@ -246,20 +290,26 @@
         scratch_shapes=sum_scratch(sizes, rows + less, size),
         compiler_params=params(1),
         name="apply",
-    )(inverse_one, panel, trailing)
-    return pl.pallas_call(
+    )(inverse_one, panel, near)
+    basis, upper, coupling_t, updated = pl.pallas_call(
         functools.partial(final_kernel, scale),
         out_shape=[
             jax.ShapeDtypeStruct((size, width), f32),
             jax.ShapeDtypeStruct((size, size), f32),
-            jax.ShapeDtypeStruct((size, trail), f32),
+            jax.ShapeDtypeStruct((trail, size), f32),
             jax.ShapeDtypeStruct((trail, width), f32),
         ],
         in_specs=[VMEM] * 5,
-        out_specs=[VMEM] * 4,
+        out_specs=[HBM, VMEM, VMEM, HBM],
+        scratch_shapes=[
+            pltpu.VMEM((size, width), f32),
+            pltpu.VMEM((trail, width), f32),
+            pltpu.SemaphoreType.DMA((2, width // chunk_of(width, 512))),
+        ],
         compiler_params=params(),
         name="final",
-    )(summed[:, :rows].reshape(size, size), summed[:, rows:].reshape(trail, size), upper_one, first, trailing)
+    )(summed[:, :rows].reshape(size, size), summed[:, rows:].reshape(trail, size), upper_one, first, near)
+    return basis, upper, coupling_t.T, updated
 
 
 def solution(mesh):

time: 62.9 us -> 44.5 us (0.71)
  Pallas kernels: 58.4 us -> 40.8 us
  local copies, waits for them, and re-layouts: 3.53 us -> 2.82 us
    pallas_call x1, Pallas kernels: 15.5 us -> 6.92 us  [shards(): pl.pallas_call(functools.partial(final_kernel, scale), out_shape=[jax.Sha...]
    pallas_call x1, Pallas kernels: 10.8 us -> 3.98 us  [shards(): pl.pallas_call(factor_kernel, out_shape=[jax.ShapeDtypeStruct((size, size...]
    pallas_call x1, Pallas kernels: 15.4 us -> 13.8 us  [shards(): pl.pallas_call(functools.partial(apply_kernel, sizes), out_shape=[jax.Sha...]
    pallas_call x1 -> x0, local copies, waits for them, and re-layouts: 0.7 us -> none  [shards(): pl.pallas_call(functools.partial(final_kernel, scale), out_shape=[jax.Sha...]
    pallas_call x1, Pallas kernels: 16.8 us -> 16.1 us  [shards(): pl.pallas_call(functools.partial(gram_kernel, sizes), out_shape=jax.Shape...]
    unnamed x8 -> x6, local copies, waits for them, and re-layouts: 2.82 us -> 2.81 us
where the time goes in v1:
time: 44.5 us; the launch traced here: 44.3 us
  Pallas kernels  40.8 us (92%)
  local copies, waits for them, and re-layouts  2.82 us (6%)
  between operations  0.69 us (2%)
    pallas_call x1, Pallas kernels, shards(): pl.pallas_call(functools.partial(gram_kernel, sizes), out_shape=jax.Shape...  16.1 us
    pallas_call x1, Pallas kernels, shards(): pl.pallas_call(functools.partial(apply_kernel, sizes), out_shape=[jax.Sha...  13.8 us
    pallas_call x1, Pallas kernels, shards(): pl.pallas_call(functools.partial(final_kernel, scale), out_shape=[jax.Sha...  6.92 us
    pallas_call x1, Pallas kernels, shards(): pl.pallas_call(factor_kernel, out_shape=[jax.ShapeDtypeStruct((size, size...  3.98 us
    unnamed x6, local copies, waits for them, and re-layouts  2.81 us

profile of v1, /device:TPU:0, one launch (start us, length us, event | category | flops | bytes accessed | tf_op | source)
XLA Modules:
  0.0 44.3 jit_solution(11399812485009323166)
XLA Ops:
  0.6 0.0 copy-start
  0.6 1.6 %copy-done = f32[128,4096]{1,0:T(8,128)S(1)} copy-done((f32[128,4096]{1,0:T(8,128)S(1)}, f32[128,4096]{1,0:T(8,128)}, u32[]{:S(2)}) %copy-start) | copy-done | bytes 2097176
  2.2 0.0 copy-start.1
  2.2 16.1 %gram.1 = f32[8,16,128]{2,1,0:T(8,128)S(1)} custom-call(f32[128,4096]{1,0:T(8,128)S(1)} %copy-done), custom_call_target="tpu_custom_call" | custom-call | tf_op jit(solution)/shard_map/gram/pallas_call | solution.py:263
  18.4 0.0 copy-start.2
  18.4 1.2 %copy-done.2 = f32[64,4096]{1,0:T(8,128)S(1)} copy-done((f32[64,4096]{1,0:T(8,128)S(1)}, f32[64,4096]{1,0:T(8,128)}, u32[]{:S(2)}) %copy-start.2) | copy-done | bytes 1048600
  19.6 4.0 %factor.1 = (f32[128,128]{1,0:T(8,128)S(1)}, f32[128,128]{1,0:T(8,128)S(1)}, f32[64,4096]{1,0:T(8,128)S(1)}) custom-call(f32[128,128]{1,0:T(8,128)S(1)} %bitcast.5, f32[64,4096]{1,0:T(8,128)S(1)} %copy-done.2), custom_call_target="tpu_custom_call" | custom-call | tf_op jit(solution)/shard_map/factor/pallas_call | solution.py:276
  23.6 0.0 copy-done.1
  23.6 13.8 %apply.1 = (f32[128,4096]{1,0:T(8,128)S(1)}, f32[8,24,128]{2,1,0:T(8,128)S(1)}) custom-call(f32[128,128]{1,0:T(8,128)S(1)} %get-tuple-element.13.inverse, f32[128,4096]{1,0:T(8,128)S(1)} %copy-done.1, f32[64,4096]{1,0:T(8,128)S(1)} %get-tuple-element.14.trailing), custom_call_target="tpu_custom_call" | custom-call | tf_op jit(solution)/shard_map/apply/pallas_call | solution.py:285
  37.4 6.9 %final.1 = (f32[128,4096]{1,0:T(8,128)}, f32[128,128]{1,0:T(8,128)}, f32[64,128]{1,0:T(8,128)}, f32[64,4096]{1,0:T(8,128)}) custom-call(f32[128,128]{1,0:T(8,128)S(1)} %bitcast.6, f32[64,128]{1,0:T(8,128)S(1)} %slice_bitcast_fusion.cross, f32[128,128]{1,0:T(8,128)S(1)} %get-tuple-element.16.upper_one, f32[128,4096]{1,0:T(8,128)S(1)} %get-tuple-element.17.first, ...), custom_call_target="tpu_custom_call" | custom-call | tf_op jit(solution)/shard_map/final/pallas_call | solution.py:294
  (2 shorter events, 0.0 us)
Async XLA Ops:
  0.6 1.6 %copy-start = (f32[128,4096]{1,0:T(8,128)S(1)}, f32[128,4096]{1,0:T(8,128)}, u32[]{:S(2)}) copy-start(f32[128,4096]{1,0:T(8,128)} %panel.3) | copy-start | bytes 6291460
  2.2 21.3 %copy-start.1 = (f32[128,4096]{1,0:T(8,128)S(1)}, f32[128,4096]{1,0:T(8,128)}, u32[]{:S(2)}) copy-start(f32[128,4096]{1,0:T(8,128)} %panel.3) | copy-start | bytes 6291460
  18.4 1.2 %copy-start.2 = (f32[64,4096]{1,0:T(8,128)S(1)}, f32[64,4096]{1,0:T(8,128)}, u32[]{:S(2)}) copy-start(f32[64,4096]{1,0:T(8,128)} %trailing.1) | copy-start | bytes 3145732

commit v2 on v1

--- a/solution.py
+++ b/solution.py
@@ -90,7 +90,6 @@
     group = nx * ny
     gx, gy, gz = lax.axis_index("gx"), lax.axis_index("gy"), lax.axis_index("gz")
     me = gx * ny + gy
-    pl.semaphore_wait(pltpu.get_barrier_semaphore(), group - 1 + nz - 1)
 
     def plane_copy(src, dst, step, base):
         peer = lax.rem(me + step, group)
@@ -155,91 +154,100 @@
     return most if width % most == 0 else width
 
 
-def gram_kernel(sizes, panel, gathered, held, load_sem, send, landed, column, send_sem, recv_sem):
+def reduce_kernel(sizes, panel, trailing, first, upper, summed, panel_held, trailing_held, first_held, move_sem, *scratch):
     size, width = panel.shape
+    trail = trailing.shape[0]
+    group = sizes[0] * sizes[1]
+    rows, less = size // group, trail // group
     chunk = chunk_of(width, 1024)
-    loads = []
+    greet(sizes)
+    loads, more, stores = [], [], []
     for i in range(width // chunk):
         at = pl.ds(i * chunk, chunk)
-        loads.append(pltpu.make_async_copy(panel.at[:, at], held.at[:, at], load_sem.at[i]))
+        loads.append(pltpu.make_async_copy(panel.at[:, at], panel_held.at[:, at], move_sem.at[0, i]))
         loads[-1].start()
-    greet(sizes)
+    for i in range(width // chunk):
+        at = pl.ds(i * chunk, chunk)
+        more.append(pltpu.make_async_copy(trailing.at[:, at], trailing_held.at[:, at], move_sem.at[1, i]))
+        more[-1].start()
     both = jnp.zeros((2 * size, 2 * size), jnp.float32)
     small = jnp.zeros((size, size), jnp.float32)
     for i in range(width // chunk):
         loads[i].wait()
-        high, middle, low = terms(held[:, i * chunk : (i + 1) * chunk], 3)
+        high, middle, low = terms(panel_held[:, i * chunk : (i + 1) * chunk], 3)
         pair = jnp.concatenate([high, middle], axis=0)
         both = both + stacked(pair, pair, NT)
         small = small + stacked(high, low, NT)
     small = small + both[:size, size:]
     gram = both[:size, :size] + ((small + small.T) + both[size:, size:])
-    group = sizes[0] * sizes[1]
-    rows = size // group
+    gathered, *first_sum = scratch[:6]
     for p in range(group):
-        send[p] = gram[p * rows : (p + 1) * rows]
-    all_sum(sizes, send, landed, column, gathered, send_sem, recv_sem)
-
-
-def factor_kernel(gram, trailing, upper, inverse, near, load_sem):
-    load = pltpu.make_async_copy(trailing, near, load_sem)
-    load.start()
-    uppers, inverses = factor([gram[h : h + 8] for h in range(0, gram.shape[0], 8)])
+        first_sum[0][p] = gram[p * rows : (p + 1) * rows]
+    pl.semaphore_wait(pltpu.get_barrier_semaphore(), group - 1 + sizes[2] - 1)
+    all_sum(sizes, first_sum[0], first_sum[1], first_sum[2], gathered, *first_sum[3:])
+    gram = jnp.concatenate([gathered[p] for p in range(group)], axis=0)
+    uppers, inverses = factor([gram[h : h + 8] for h in range(0, size, 8)])
     for h in range(len(uppers)):
         upper[8 * h : 8 * h + 8] = uppers[h]
-        inverse[8 * h : 8 * h + 8] = inverses[h]
-    load.wait()
-
-
-def apply_kernel(sizes, inverse, panel, trailing, first, gathered, send, landed, column, send_sem, recv_sem):
-    greet(sizes)
-    size, width = panel.shape
-    trail = trailing.shape[0]
-    chunk = chunk_of(width, 1024)
-    one, two, three = terms(inverse[...], 3)
+    inverse = jnp.concatenate(inverses, axis=0)
+    one, two, three = terms(inverse, 3)
     left = jnp.concatenate([three, one, two, two, one, one], axis=1)
-
-    def body(i, total):
-        at = pl.ds(pl.multiple_of(i * chunk, chunk), chunk)
-        high, middle, low = terms(panel[:, at], 3)
+    total = jnp.zeros((size + 2 * trail, 2 * size), jnp.float32)
+    for i in range(width // chunk):
+        at = pl.ds(i * chunk, chunk)
+        high, middle, low = terms(panel_held[:, at], 3)
         basis = stacked(left, jnp.concatenate([high, low, middle, high, middle, high], axis=0), NN)
-        first[:, at] = basis
+        first_held[:, at] = basis
+        stores.append(pltpu.make_async_copy(first_held.at[:, at], first.at[:, at], move_sem.at[2, i]))
+        stores[-1].start()
         high, low = terms(basis, 2)
-        c_high, c_low = terms(trailing[:, at], 2)
-        pairs = stacked(jnp.concatenate([high, c_high, c_low], axis=0), jnp.concatenate([high, low], axis=0), NT)
-        return total + pairs
-
-    total = lax.fori_loop(0, width // chunk, body, jnp.zeros((size + 2 * trail, 2 * size), jnp.float32))
+        more[i].wait()
+        c_high, c_low = terms(trailing_held[:, at], 2)
+        left_terms = jnp.concatenate([high, c_high, c_low], axis=0)
+        total = total + stacked(left_terms, jnp.concatenate([high, low], axis=0), NT)
     mixed = total[:size, size:]
     own = total[:size, :size] + (mixed + mixed.T)
     cross = total[size:, :size] + total[size:, size:]
     cross = cross[:trail] + cross[trail:]
-    group = sizes[0] * sizes[1]
-    rows, less = size // group, trail // group
+    second_sum = scratch[6:]
     for p in range(group):
-        send[p, :rows] = own[p * rows : (p + 1) * rows]
-        send[p, rows:] = cross[p * less : (p + 1) * less]
-    all_sum(sizes, send, landed, column, gathered, send_sem, recv_sem)
-
-
-def final_kernel(scale, gram, cross, upper_one, first, trailing, basis, upper, coupling, updated, basis_held, updated_held, store_sem):
+        second_sum[0][p, :rows] = own[p * rows : (p + 1) * rows]
+        second_sum[0][p, rows:] = cross[p * less : (p + 1) * less]
+    all_sum(sizes, second_sum[0], second_sum[1], second_sum[2], summed, *second_sum[3:])
+    for store in stores:
+        store.wait()
+
+
+def final_kernel(scale, summed, upper_one, first, trailing, basis, upper, coupling, updated, first_held, trailing_held, basis_held, updated_held, load_sem, store_sem):
     size, width = first.shape
+    loads = [
+        pltpu.make_async_copy(first, first_held, load_sem.at[0]),
+        pltpu.make_async_copy(trailing, trailing_held, load_sem.at[1]),
+    ]
+    for load in loads:
+        load.start()
+    group = summed.shape[0]
+    rows = size // group
+    gram = jnp.concatenate([summed[p, :rows] for p in range(group)], axis=0)
+    cross = jnp.concatenate([summed[p, rows:] for p in range(group)], axis=0)
     uppers, inverses = factor([gram[h : h + 8] for h in range(0, size, 8)])
     inv = jnp.concatenate(inverses, axis=0)
     up = jnp.concatenate(uppers, axis=0)
-    mixed = exact(cross[...], inv, NT)
+    mixed = exact(cross, inv, NT)
     coupling[...] = mixed
     both = jnp.concatenate([inv * scale, exact(mixed, inv, NN)], axis=0)
     high, low = terms(both, 2)
     left = jnp.concatenate([low, low, high, high], axis=1)
     chunk = chunk_of(width, 512)
     stores = []
+    for load in loads:
+        load.wait()
     for i in range(width // chunk):
         at = pl.ds(i * chunk, chunk)
-        high, low = terms(first[:, at], 2)
+        high, low = terms(first_held[:, at], 2)
         out = stacked(left, jnp.concatenate([low, high, low, high], axis=0), NN)
         basis_held[:, at] = out[:size]
-        updated_held[:, at] = trailing[:, at] - out[size:]
+        updated_held[:, at] = trailing_held[:, at] - out[size:]
         for place, (src, dst) in enumerate(((basis_held, basis), (updated_held, updated))):
             stores.append(pltpu.make_async_copy(src.at[:, at], dst.at[:, at], store_sem.at[place, i]))
             stores[-1].start()
@@ -257,40 +265,32 @@
     f32 = jnp.float32
     scale = float(width * group * nz) ** 0.5
 
-    def params(identity=None):
-        return pltpu.CompilerParams(collective_id=identity, has_side_effects=identity is not None, vmem_limit_bytes=48 * 2**20)
-
-    gram = pl.pallas_call(
-        functools.partial(gram_kernel, sizes),
-        out_shape=jax.ShapeDtypeStruct((group, rows, size), f32),
-        in_specs=[HBM],
-        out_specs=VMEM,
+    def params(identity=None, mebibytes=63):
+        return pltpu.CompilerParams(
+            collective_id=identity, has_side_effects=identity is not None, vmem_limit_bytes=mebibytes * 2**20
+        )
+
+    first, upper_one, summed = pl.pallas_call(
+        functools.partial(reduce_kernel, sizes),
+        out_shape=[
+            jax.ShapeDtypeStruct((size, width), f32),
+            jax.ShapeDtypeStruct((size, size), f32),
+            jax.ShapeDtypeStruct((group, rows + less, size), f32),
+        ],
+        in_specs=[HBM, HBM],
+        out_specs=[HBM, VMEM, VMEM],
         scratch_shapes=[
             pltpu.VMEM((size, width), f32),
-            pltpu.SemaphoreType.DMA((width // chunk_of(width, 1024),)),
+            pltpu.VMEM((trail, width), f32),
+            pltpu.VMEM((size, width), f32),
+            pltpu.SemaphoreType.DMA((3, width // chunk_of(width, 1024))),
+            pltpu.VMEM((group, rows, size), f32),
             *sum_scratch(sizes, rows, size),
+            *sum_scratch(sizes, rows + less, size),
         ],
         compiler_params=params(0),
-        name="gram",
-    )(panel)
-    upper_one, inverse_one, near = pl.pallas_call(
-        factor_kernel,
-        out_shape=[jax.ShapeDtypeStruct((size, size), f32)] * 2 + [jax.ShapeDtypeStruct((trail, width), f32)],
-        in_specs=[VMEM, HBM],
-        out_specs=[VMEM] * 3,
-        scratch_shapes=[pltpu.SemaphoreType.DMA],
-        compiler_params=params(),
-        name="factor",
-    )(gram.reshape(size, size), trailing)
-    first, summed = pl.pallas_call(
-        functools.partial(apply_kernel, sizes),
-        out_shape=[jax.ShapeDtypeStruct((size, width), f32), jax.ShapeDtypeStruct((group, rows + less, size), f32)],
-        in_specs=[VMEM] * 3,
-        out_specs=[VMEM] * 2,
-        scratch_shapes=sum_scratch(sizes, rows + less, size),
-        compiler_params=params(1),
-        name="apply",
-    )(inverse_one, panel, near)
+        name="reduce",
+    )(panel, trailing)
     basis, upper, coupling_t, updated = pl.pallas_call(
         functools.partial(final_kernel, scale),
         out_shape=[
@@ -299,16 +299,19 @@
             jax.ShapeDtypeStruct((trail, size), f32),
             jax.ShapeDtypeStruct((trail, width), f32),
         ],
-        in_specs=[VMEM] * 5,
+        in_specs=[VMEM, VMEM, HBM, HBM],
         out_specs=[HBM, VMEM, VMEM, HBM],
         scratch_shapes=[
             pltpu.VMEM((size, width), f32),
             pltpu.VMEM((trail, width), f32),
+            pltpu.VMEM((size, width), f32),
+            pltpu.VMEM((trail, width), f32),
+            pltpu.SemaphoreType.DMA((2,)),
             pltpu.SemaphoreType.DMA((2, width // chunk_of(width, 512))),
         ],
         compiler_params=params(),
         name="final",
-    )(summed[:, :rows].reshape(size, size), summed[:, rows:].reshape(trail, size), upper_one, first, near)
+    )(summed, upper_one, first, trailing)
     return basis, upper, coupling_t.T, updated
 
 

time: 44.5 us -> 43.5 us (0.978)
  local copies, waits for them, and re-layouts: 2.82 us -> 0 us
  Pallas kernels: 40.8 us -> 42.7 us
    unnamed x6 -> x0, local copies, waits for them, and re-layouts: 2.81 us -> none
    pallas_call x1, Pallas kernels: 6.92 us -> 8.82 us  [shards(): pl.pallas_call(functools.partial(final_kernel, scale), out_shape=[jax.Sha...]
    pallas_call x3 -> x1, Pallas kernels: 33.9 us -> 33.8 us  [shards(): pl.pallas_call(functools.partial(reduce_kernel, sizes), out_shape=[jax.Sh...]
where the time goes in v2:
time: 43.5 us; the launch traced here: 43.3 us
  Pallas kernels  42.7 us (98%)
  between operations  0.64 us (1%)
    pallas_call x1, Pallas kernels, shards(): pl.pallas_call(functools.partial(reduce_kernel, sizes), out_shape=[jax.Sh...  33.8 us
    pallas_call x1, Pallas kernels, shards(): pl.pallas_call(functools.partial(final_kernel, scale), out_shape=[jax.Sha...  8.82 us

profile of v2, /device:TPU:0, one launch (start us, length us, event | category | flops | bytes accessed | tf_op | source)
XLA Modules:
  0.0 43.3 jit_solution(14051308434627400272)
XLA Ops:
  0.6 33.8 %reduce.1 = (f32[128,4096]{1,0:T(8,128)}, f32[128,128]{1,0:T(8,128)}, f32[8,24,128]{2,1,0:T(8,128)}) custom-call(f32[128,4096]{1,0:T(8,128)} %panel.1, f32[64,4096]{1,0:T(8,128)} %trailing.3), custom_call_target="tpu_custom_call" | custom-call | tf_op jit(solution)/shard_map/reduce/pallas_call | solution.py:273
  34.5 8.8 %final.1 = (f32[128,4096]{1,0:T(8,128)}, f32[128,128]{1,0:T(8,128)}, f32[64,128]{1,0:T(8,128)}, f32[64,4096]{1,0:T(8,128)}) custom-call(f32[8,24,128]{2,1,0:T(8,128)} %get-tuple-element.11.summed, f32[128,128]{1,0:T(8,128)} %get-tuple-element.12.upper_one, f32[128,4096]{1,0:T(8,128)} %get-tuple-element.13.first, f32[64,4096]{1,0:T(8,128)} %trailing.3), custom_call_target="tpu_custom_call" | custom-call | tf_op jit(solution)/shard_map/final/pallas_call | solution.py:294

commit v3 on v2

--- a/solution.py
+++ b/solution.py
@@ -154,7 +154,7 @@
     return most if width % most == 0 else width
 
 
-def reduce_kernel(sizes, panel, trailing, first, upper, summed, panel_held, trailing_held, first_held, move_sem, *scratch):
+def reduce_kernel(sizes, panel, trailing, first, upper, summed, panel_held, trailing_held, first_held, move_sem, upper_held, *scratch):
     size, width = panel.shape
     trail = trailing.shape[0]
     group = sizes[0] * sizes[1]
@@ -188,7 +188,9 @@
     gram = jnp.concatenate([gathered[p] for p in range(group)], axis=0)
     uppers, inverses = factor([gram[h : h + 8] for h in range(0, size, 8)])
     for h in range(len(uppers)):
-        upper[8 * h : 8 * h + 8] = uppers[h]
+        upper_held[8 * h : 8 * h + 8] = uppers[h]
+    stores.append(pltpu.make_async_copy(upper_held, upper, move_sem.at[3, 0]))
+    stores[-1].start()
     inverse = jnp.concatenate(inverses, axis=0)
     one, two, three = terms(inverse, 3)
     left = jnp.concatenate([three, one, two, two, one, one], axis=1)
@@ -218,11 +220,12 @@
         store.wait()
 
 
-def final_kernel(scale, summed, upper_one, first, trailing, basis, upper, coupling, updated, first_held, trailing_held, basis_held, updated_held, load_sem, store_sem):
+def final_kernel(scale, summed, upper_one, first, trailing, basis, upper, coupling, updated, first_held, trailing_held, basis_held, updated_held, one_held, upper_held, coupling_held, load_sem, store_sem):
     size, width = first.shape
     loads = [
         pltpu.make_async_copy(first, first_held, load_sem.at[0]),
         pltpu.make_async_copy(trailing, trailing_held, load_sem.at[1]),
+        pltpu.make_async_copy(upper_one, one_held, load_sem.at[2]),
     ]
     for load in loads:
         load.start()
@@ -234,14 +237,18 @@
     inv = jnp.concatenate(inverses, axis=0)
     up = jnp.concatenate(uppers, axis=0)
     mixed = exact(cross, inv, NT)
-    coupling[...] = mixed
+    coupling_held[...] = mixed
     both = jnp.concatenate([inv * scale, exact(mixed, inv, NN)], axis=0)
     high, low = terms(both, 2)
     left = jnp.concatenate([low, low, high, high], axis=1)
     chunk = chunk_of(width, 512)
-    stores = []
+    stores = [pltpu.make_async_copy(coupling_held, coupling, load_sem.at[3])]
+    stores[0].start()
     for load in loads:
         load.wait()
+    upper_held[...] = exact(up, one_held[...], NN) * (1.0 / scale)
+    stores.append(pltpu.make_async_copy(upper_held, upper, load_sem.at[4]))
+    stores[-1].start()
     for i in range(width // chunk):
         at = pl.ds(i * chunk, chunk)
         high, low = terms(first_held[:, at], 2)
@@ -251,7 +258,6 @@
         for place, (src, dst) in enumerate(((basis_held, basis), (updated_held, updated))):
             stores.append(pltpu.make_async_copy(src.at[:, at], dst.at[:, at], store_sem.at[place, i]))
             stores[-1].start()
-    upper[...] = exact(up, upper_one[...], NN) * (1.0 / scale)
     for store in stores:
         store.wait()
 
@@ -265,7 +271,7 @@
     f32 = jnp.float32
     scale = float(width * group * nz) ** 0.5
 
-    def params(identity=None, mebibytes=63):
+    def params(identity=None, mebibytes=53):
         return pltpu.CompilerParams(
             collective_id=identity, has_side_effects=identity is not None, vmem_limit_bytes=mebibytes * 2**20
         )
@@ -278,12 +284,13 @@
             jax.ShapeDtypeStruct((group, rows + less, size), f32),
         ],
         in_specs=[HBM, HBM],
-        out_specs=[HBM, VMEM, VMEM],
+        out_specs=[HBM, HBM, VMEM],
         scratch_shapes=[
             pltpu.VMEM((size, width), f32),
             pltpu.VMEM((trail, width), f32),
             pltpu.VMEM((size, width), f32),
-            pltpu.SemaphoreType.DMA((3, width // chunk_of(width, 1024))),
+            pltpu.SemaphoreType.DMA((4, width // chunk_of(width, 1024))),
+            pltpu.VMEM((size, size), f32),
             pltpu.VMEM((group, rows, size), f32),
             *sum_scratch(sizes, rows, size),
             *sum_scratch(sizes, rows + less, size),
@@ -299,14 +306,17 @@
             jax.ShapeDtypeStruct((trail, size), f32),
             jax.ShapeDtypeStruct((trail, width), f32),
         ],
-        in_specs=[VMEM, VMEM, HBM, HBM],
-        out_specs=[HBM, VMEM, VMEM, HBM],
+        in_specs=[VMEM, HBM, HBM, HBM],
+        out_specs=[HBM] * 4,
         scratch_shapes=[
             pltpu.VMEM((size, width), f32),
             pltpu.VMEM((trail, width), f32),
             pltpu.VMEM((size, width), f32),
             pltpu.VMEM((trail, width), f32),
-            pltpu.SemaphoreType.DMA((2,)),
+            pltpu.VMEM((size, size), f32),
+            pltpu.VMEM((size, size), f32),
+            pltpu.VMEM((trail, size), f32),
+            pltpu.SemaphoreType.DMA((5,)),
             pltpu.SemaphoreType.DMA((2, width // chunk_of(width, 512))),
         ],
         compiler_params=params(),

time: 43.5 us -> 40.8 us (0.938)
  Pallas kernels: 42.7 us -> 40 us
    pallas_call x1, Pallas kernels: 8.82 us -> 6.62 us  [shards(): pl.pallas_call(functools.partial(final_kernel, scale), out_shape=[jax.Sha...]
where the time goes in v3:
time: 40.8 us; the launch traced here: 40.7 us
  Pallas kernels  40 us (98%)
  between operations  0.64 us (2%)
    pallas_call x1, Pallas kernels, shards(): pl.pallas_call(functools.partial(reduce_kernel, sizes), out_shape=[jax.Sh...  33.4 us
    pallas_call x1, Pallas kernels, shards(): pl.pallas_call(functools.partial(final_kernel, scale), out_shape=[jax.Sha...  6.62 us

profile of v3, /device:TPU:0, one launch (start us, length us, event | category | flops | bytes accessed | tf_op | source)
XLA Modules:
  0.0 40.7 jit_solution(2273608505369922137)
XLA Ops:
  0.6 33.4 %reduce.1 = (f32[128,4096]{1,0:T(8,128)}, f32[128,128]{1,0:T(8,128)S(1)}, f32[8,24,128]{2,1,0:T(8,128)S(1)}) custom-call(f32[128,4096]{1,0:T(8,128)} %panel.1, f32[64,4096]{1,0:T(8,128)} %trailing.3), custom_call_target="tpu_custom_call" | custom-call | tf_op jit(solution)/shard_map/reduce/pallas_call | solution.py:279
  34.0 6.6 %final.1 = (f32[128,4096]{1,0:T(8,128)}, f32[128,128]{1,0:T(8,128)}, f32[64,128]{1,0:T(8,128)}, f32[64,4096]{1,0:T(8,128)}) custom-call(f32[8,24,128]{2,1,0:T(8,128)S(1)} %get-tuple-element.11.summed, f32[128,128]{1,0:T(8,128)S(1)} %get-tuple-element.12.upper_one, f32[128,4096]{1,0:T(8,128)} %get-tuple-element.13.first, f32[64,4096]{1,0:T(8,128)} %trailing.3), custom_call_target="tpu_custom_call" | custom-call | tf_op jit(solution)/shard_map/final/pallas_call | solution.py:301

commit v4 on v3

--- a/solution.py
+++ b/solution.py
@@ -160,7 +160,6 @@
     group = sizes[0] * sizes[1]
     rows, less = size // group, trail // group
     chunk = chunk_of(width, 1024)
-    greet(sizes)
     loads, more, stores = [], [], []
     for i in range(width // chunk):
         at = pl.ds(i * chunk, chunk)
@@ -170,6 +169,7 @@
         at = pl.ds(i * chunk, chunk)
         more.append(pltpu.make_async_copy(trailing.at[:, at], trailing_held.at[:, at], move_sem.at[1, i]))
         more[-1].start()
+    greet(sizes)
     both = jnp.zeros((2 * size, 2 * size), jnp.float32)
     small = jnp.zeros((size, size), jnp.float32)
     for i in range(width // chunk):

time: 40.8 us -> 40.8 us (level)
  no operation moved by 1% of the time
where the time goes in v4:
time: 40.8 us; the launch traced here: 40.7 us
  Pallas kernels  40 us (98%)
  between operations  0.64 us (2%)
    pallas_call x1, Pallas kernels, shards(): pl.pallas_call(functools.partial(reduce_kernel, sizes), out_shape=[jax.Sh...  33.4 us
    pallas_call x1, Pallas kernels, shards(): pl.pallas_call(functools.partial(final_kernel, scale), out_shape=[jax.Sha...  6.62 us

profile of v4, /device:TPU:0, one launch (start us, length us, event | category | flops | bytes accessed | tf_op | source)
XLA Modules:
  0.0 40.7 jit_solution(8078212843277403076)
XLA Ops:
  0.6 33.4 %reduce.1 = (f32[128,4096]{1,0:T(8,128)}, f32[128,128]{1,0:T(8,128)S(1)}, f32[8,24,128]{2,1,0:T(8,128)S(1)}) custom-call(f32[128,4096]{1,0:T(8,128)} %panel.1, f32[64,4096]{1,0:T(8,128)} %trailing.3), custom_call_target="tpu_custom_call" | custom-call | tf_op jit(solution)/shard_map/reduce/pallas_call | solution.py:279
  34.1 6.6 %final.1 = (f32[128,4096]{1,0:T(8,128)}, f32[128,128]{1,0:T(8,128)}, f32[64,128]{1,0:T(8,128)}, f32[64,4096]{1,0:T(8,128)}) custom-call(f32[8,24,128]{2,1,0:T(8,128)S(1)} %get-tuple-element.11.summed, f32[128,128]{1,0:T(8,128)S(1)} %get-tuple-element.12.upper_one, f32[128,4096]{1,0:T(8,128)} %get-tuple-element.13.first, f32[64,4096]{1,0:T(8,128)} %trailing.3), custom_call_target="tpu_custom_call" | custom-call | tf_op jit(solution)/shard_map/final/pallas_call | solution.py:301
